TPU v7x, 256 devices: a whole 4x4x8 slice. The times are simulated.
256 devices in a mesh: dp: 2 (over core), seq: 8 (over z), expert: 16 (over y, x).
Axes of the slice: x: 4, y: 4, z: 8, core: 2. Of those that a mesh axis runs over, the one named last changes fastest.
Arguments:
- tokens: bfloat16 [16384, 2048], P(('dp', 'seq')), may hold values from -6 to 6
- phi: bfloat16 [2048, 32], P(None, 'expert'), may hold values from -40 to 40
- w_in: bfloat16 [32, 2048, 8192], P('expert', None, ('dp', 'seq')), may hold values from -1 to 1
- w_out: bfloat16 [32, 8192, 2048], P('expert', ('dp', 'seq')), may hold values from -0.25 to 0.25
Outputs:
- mixed: bfloat16 [16384, 2048], P(('dp', 'seq', 'expert'))
All inputs are finite; a program needn't handle non-finite values.
Results may differ from a plain program's by a relative error of at most 0.0068.
Values may be sent and summed in bfloat16 or wider, within the bound.
A program may use at most 64 MiB of HBM per device.

v0:
```python
import jax
import jax.numpy as jnp
from jax import lax
from jax.sharding import PartitionSpec as P


def on_device(tokens, phi, w_in, w_out):
    logits = lax.dot_general(
        phi, tokens, (((0,), (1,)), ((), ())), preferred_element_type=jnp.float32
    )
    slot_max = lax.pmax(jnp.max(logits, axis=1), "seq")
    spread = jnp.exp(logits - slot_max[:, None])
    numerator = jnp.dot(spread.astype(jnp.bfloat16), tokens, preferred_element_type=jnp.float32)
    denominator = jnp.sum(spread, axis=1)
    numer_seq, denom_seq = lax.psum((numerator, denominator), "seq")
    own_slots = (numer_seq / denom_seq[:, None]).astype(jnp.bfloat16)
    slot_in = lax.all_gather(own_slots[None], "dp", axis=0, tiled=True)
    hidden = jax.nn.gelu(
        jnp.einsum("ced,edf->cef", slot_in, w_in, preferred_element_type=jnp.float32),
        approximate=True,
    ).astype(jnp.bfloat16)
    partial_value = jnp.einsum("cef,efd->ced", hidden, w_out, preferred_element_type=jnp.float32)
    totals = lax.psum(partial_value, ("dp", "seq"))
    summed = lax.dynamic_index_in_dim(totals, lax.axis_index("dp"), 0, keepdims=False)
    slot_out = summed.astype(jnp.bfloat16)
    row_max = lax.pmax(jnp.max(logits, axis=0), "expert")
    combine_weights = jnp.exp(logits - row_max[None, :])
    local_numer = lax.dot_general(
        combine_weights.astype(jnp.bfloat16),
        slot_out,
        (((0,), (0,)), ((), ())),
        preferred_element_type=jnp.float32,
    )
    mixed_numer, mixed_denom = (
        lax.psum_scatter(local_numer, "expert", scatter_dimension=0, tiled=True),
        lax.psum_scatter(
            jnp.sum(combine_weights, axis=0), "expert", scatter_dimension=0, tiled=True
        ),
    )
    return (mixed_numer / mixed_denom[:, None]).astype(jnp.bfloat16)


def solution(mesh):
    placed = (
        P(("dp", "seq"), None),
        P(None, "expert"),
        P("expert", None, ("dp", "seq")),
        P("expert", ("dp", "seq"), None),
    )
    return jax.shard_map(
        on_device,
        mesh=mesh,
        in_specs=placed,
        out_specs=P(("dp", "seq", "expert"), None),
        check_vma=False,
    )
```

profile of v0, /device:TPU:2, one launch (start us, length us, event | category | flops | bytes accessed | tf_op | source)
XLA Modules:
  0.0 258.3 jit_solution(14364468299653725748)
XLA Ops:
  6.5 0.0 copy-start
  6.5 0.0 reduce-scatter.2.cloned.1.call-start
  6.5 0.7 copy-done
  7.2 3.5 %fusion.35 = (f32[1024]{0:T(1024)S(1)}, f32[2]{0:T(128)S(1)}, f32[2,1024]{1,0:T(2,128)S(1)}) fusion(bf16[2048,2]{0,1:T(2,128)(2,1)S(1)} %copy-done, bf16[1024,2048]{1,0:T(8,128)(2,1)} %param.4), kind=kOutput, calls=%fused_computation.35 | convolution fusion | flops 8391678 | bytes 4214792 | tf_op jit(solution)/shard_map/dot_general | solution.py:8
  10.7 37.7 %pmax.14 = f32[1024]{0:T(1024)S(1)} all-reduce(f32[1024]{0:T(1024)S(1)} %get-tuple-element.7), channel_id=1, replica_groups=mesh['dp'=2,'seq'=8,'expert'=16] {'expert'}, use_global_device_ids=true, to_apply=%region_1.0 | all-reduce | flops 1024 | bytes 8192 | tf_op jit(solution)/shard_map/pmax | solution.py:26
  48.4 19.0 %pmax.15 = f32[2]{0:T(128)S(1)} all-reduce(f32[2]{0:T(128)S(1)} %get-tuple-element.8), channel_id=1, replica_groups=mesh['dp'=2,'seq'=8,'expert'=16] {'seq'}, use_global_device_ids=true, to_apply=%region_3.0 | all-reduce | flops 2 | bytes 16 | tf_op jit(solution)/shard_map/pmax | solution.py:11
  67.4 2.9 %fusion.23 = f32[2,2048]{1,0:T(2,128)S(1)} fusion(bf16[1024,2048]{1,0:T(8,128)(2,1)} %param.4, f32[2,1024]{1,0:T(2,128)S(1)} %get-tuple-element.11, f32[2]{0:T(128)S(1)} %pmax.15), kind=kOutput, calls=%fused_computation.25 | convolution fusion | flops 8392704 | bytes 4218888 | tf_op jit(solution)/shard_map/dot_general | solution.py:13
  70.3 0.2 fusion.19
  70.5 27.1 %all-reduce.1 = (f32[2,2048]{1,0:T(2,128)S(1)}, f32[2]{0:T(128)S(1)}) all-reduce(f32[2,2048]{1,0:T(2,128)S(1)} %fusion.23, f32[2]{0:T(128)S(1)} %get-tuple-element.6), channel_id=1, replica_groups=mesh['dp'=2,'seq'=8,'expert'=16] {'seq'}, use_global_device_ids=true, to_apply=%region_4.0 | all-reduce | flops 4098 | bytes 32784 | tf_op jit(solution)/shard_map/psum | solution.py:15
  97.6 0.1 fusion.18
  97.6 1.8 all-gather.1
  99.4 4.7 %convolution_bitcast_fusion = f32[2,2,2048]{2,0,1:T(2,128)S(1)} fusion(bf16[2,512,2048]{2,1,0:T(8,128)(2,1)} %param.7, bf16[2,2048,512]{2,1,0:T(8,128)(2,1)} %param.6, bf16[2,2,2048]{2,1,0:T(2,128)(2,1)S(1)} %all-gather.1), kind=kOutput, calls=%fused_computation | convolution fusion | flops 16795648 | bytes 8437760 | tf_op jit(solution)/shard_map/cef,efd->ced/dot_general | solution.py:22
  104.1 50.2 %psum.23 = bf16[2,2,2048]{2,0,1:T(2,128)(2,1)S(1)} all-reduce(f32[2,2,2048]{2,0,1:T(2,128)S(1)} %convolution_bitcast_fusion), channel_id=1, replica_groups=mesh['dp'=2,'seq'=8,'expert'=16] {'dp','seq'}, use_global_device_ids=true, to_apply=%region_7.8 | all-reduce | flops 8192 | bytes 49152 | tf_op jit(solution)/shard_map/psum | solution.py:23
  154.3 4.5 %fusion.15 = f32[1024,2048]{1,0:T(8,128)} fusion(bf16[1,2,2048]{2,0,1:T(2,128)(2,1)S(1)} %dynamic-slice_convert_fusion, f32[2,1024]{1,0:T(2,128)S(1)} %get-tuple-element.11, f32[1024]{0:T(1024)S(1)} %pmax.14), kind=kOutput, calls=%fused_computation.15 | convolution fusion | flops 8392704 | bytes 8409088 | tf_op jit(solution)/shard_map/dot_general | solution.py:28
  158.9 0.0 copy-start.1
  158.9 0.0 reduce-scatter.2.cloned.1.call-update
  158.9 0.6 copy-done.1
  159.5 0.6 dynamic-slice
  160.8 40.2 %all-reduce = f32[1024]{0:T(1024)S(1)} all-reduce(f32[1024]{0:T(1024)S(1)} %get-tuple-element.5), channel_id=4, replica_groups=mesh['dp'=2,'seq'=8,'expert'=16] {'expert'}, use_global_device_ids=true, to_apply=%region_10.11.clone | all-reduce | flops 1024 | bytes 8192
  201.0 0.1 dynamic-slice.1
  201.1 48.5 %reduce-scatter.2.cloned.1.call-done = f32[64,2048]{1,0:T(8,128)} async-done(((f32[1024,2048]{1,0:T(8,128)}), f32[64,2048]{1,0:T(8,128)}) %reduce-scatter.2.cloned.1.call-update) | async-done | bytes 524304 | tf_op jit(solution)/shard_map/reduce_scatter | solution.py:35
  249.6 1.8 divide_convert_fusion
  (1 shorter events, 0.0 us)
Async XLA Ops:
  6.5 0.7 copy-start
  6.5 243.0 %reduce-scatter.2.cloned.1.call-start = ((), (), s32[]{:S(2)}) async-start(), calls=%async_computation.1 | async-start | bytes 8912896 | tf_op jit(solution)/shard_map/reduce_scatter | solution.py:35
  158.9 0.7 copy-start.1
Sparse Core Ops, SparseCore 0:
  159.0 90.5 reduce-scatter.1
where the time goes:
time: 259 us; the launch traced here: 258 us
  blocking collectives  176 us (68%)
  waiting for transfers between devices  48.5 us (19%)
  matrix products  15.6 us (6%)
  between operations  14.1 us (5%)
    psum x1, blocking collectives, on_device(): totals = lax.psum(partial_value, ('dp', 'seq'))  50.2 us
    reduce_scatter x1, waiting for transfers between devices, on_device(): lax.psum_scatter(local_numer, 'expert', scatter_dimension=0, tiled=True)  48.5 us
    unnamed x1, blocking collectives  40.2 us
    pmax x1, blocking collectives, on_device(): row_max = lax.pmax(jnp.max(logits, axis=0), 'expert')  37.7 us
    psum x1, blocking collectives, on_device(): numer_seq, denom_seq = lax.psum((numerator, denominator), 'seq')  27.1 us
    pmax x1, blocking collectives, on_device(): slot_max = lax.pmax(jnp.max(logits, axis=1), 'seq')  19 us
  transfers between devices with their start and end apart: 1, of which 1 were waited for; matrix products, arithmetic and copies ran while one was open for 0% of the time, Pallas kernels for 0%

commit v1 on v0

--- a/solution.py
+++ b/solution.py
@@ -20,7 +20,7 @@
         approximate=True,
     ).astype(jnp.bfloat16)
     partial_value = jnp.einsum("cef,efd->ced", hidden, w_out, preferred_element_type=jnp.float32)
-    totals = lax.psum(partial_value, ("dp", "seq"))
+    totals = lax.psum(lax.psum(partial_value, "dp"), "seq")
     summed = lax.dynamic_index_in_dim(totals, lax.axis_index("dp"), 0, keepdims=False)
     slot_out = summed.astype(jnp.bfloat16)
     row_max = lax.pmax(jnp.max(logits, axis=0), "expert")

time: 259 us -> 236 us (0.911)
  blocking collectives: 176 us -> 157 us
  waiting for transfers between devices: 48.5 us -> 45.1 us
    psum x1 -> x2, blocking collectives: 50.2 us -> 31 us  [on_device(): totals = lax.psum(lax.psum(partial_value, 'dp'), 'seq')]
    reduce_scatter x1, waiting for transfers between devices: 48.5 us -> 45.1 us  [on_device(): lax.psum_scatter(local_numer, 'expert', scatter_dimension=0, tiled=True)]
where the time goes in v1:
time: 236 us
  blocking collectives  157 us (67%)
  waiting for transfers between devices  45.1 us (19%)
  matrix products  15.6 us (7%)
  between operations  14.1 us (6%)
    reduce_scatter x1, waiting for transfers between devices, on_device(): lax.psum_scatter(local_numer, 'expert', scatter_dimension=0, tiled=True)  45.1 us
    unnamed x1, blocking collectives  40.5 us
    pmax x1, blocking collectives, on_device(): row_max = lax.pmax(jnp.max(logits, axis=0), 'expert')  37.7 us
    psum x2, blocking collectives, on_device(): totals = lax.psum(lax.psum(partial_value, 'dp'), 'seq')  31 us
    psum x1, blocking collectives, on_device(): numer_seq, denom_seq = lax.psum((numerator, denominator), 'seq')  27.1 us
    pmax x1, blocking collectives, on_device(): slot_max = lax.pmax(jnp.max(logits, axis=1), 'seq')  19 us
  transfers between devices with their start and end apart: 1, of which 1 were waited for; matrix products, arithmetic and copies ran while one was open for 0% of the time, Pallas kernels for 0%

profile of v1, /device:TPU:2, one launch (start us, length us, event | category | flops | bytes accessed | tf_op | source)
XLA Modules:
  0.0 235.9 jit_solution(13495031032659298869)
XLA Ops:
  6.5 0.0 copy-start
  6.5 0.0 reduce-scatter.2.cloned.1.call-start
  6.5 0.7 copy-done
  7.2 3.5 %fusion.35 = (f32[1024]{0:T(1024)S(1)}, f32[2]{0:T(128)S(1)}, f32[2,1024]{1,0:T(2,128)S(1)}) fusion(bf16[2048,2]{0,1:T(2,128)(2,1)S(1)} %copy-done, bf16[1024,2048]{1,0:T(8,128)(2,1)} %param.4), kind=kOutput, calls=%fused_computation.35 | convolution fusion | flops 8391678 | bytes 4214792 | tf_op jit(solution)/shard_map/dot_general | solution.py:8
  10.7 37.7 %pmax.14 = f32[1024]{0:T(1024)S(1)} all-reduce(f32[1024]{0:T(1024)S(1)} %get-tuple-element.7), channel_id=1, replica_groups=mesh['dp'=2,'seq'=8,'expert'=16] {'expert'}, use_global_device_ids=true, to_apply=%region_1.0 | all-reduce | flops 1024 | bytes 8192 | tf_op jit(solution)/shard_map/pmax | solution.py:26
  48.4 19.0 %pmax.15 = f32[2]{0:T(128)S(1)} all-reduce(f32[2]{0:T(128)S(1)} %get-tuple-element.8), channel_id=1, replica_groups=mesh['dp'=2,'seq'=8,'expert'=16] {'seq'}, use_global_device_ids=true, to_apply=%region_3.0 | all-reduce | flops 2 | bytes 16 | tf_op jit(solution)/shard_map/pmax | solution.py:11
  67.4 2.9 %fusion.23 = f32[2,2048]{1,0:T(2,128)S(1)} fusion(bf16[1024,2048]{1,0:T(8,128)(2,1)} %param.4, f32[2,1024]{1,0:T(2,128)S(1)} %get-tuple-element.11, f32[2]{0:T(128)S(1)} %pmax.15), kind=kOutput, calls=%fused_computation.25 | convolution fusion | flops 8392704 | bytes 4218888 | tf_op jit(solution)/shard_map/dot_general | solution.py:13
  70.3 0.2 fusion.19
  70.5 27.1 %all-reduce.1 = (f32[2,2048]{1,0:T(2,128)S(1)}, f32[2]{0:T(128)S(1)}) all-reduce(f32[2,2048]{1,0:T(2,128)S(1)} %fusion.23, f32[2]{0:T(128)S(1)} %get-tuple-element.6), channel_id=1, replica_groups=mesh['dp'=2,'seq'=8,'expert'=16] {'seq'}, use_global_device_ids=true, to_apply=%region_4.0 | all-reduce | flops 4098 | bytes 32784 | tf_op jit(solution)/shard_map/psum | solution.py:15
  97.6 0.1 fusion.18
  97.6 1.8 all-gather.1
  99.4 4.7 %convolution_bitcast_fusion = f32[2,2,2048]{2,0,1:T(2,128)S(1)} fusion(bf16[2,512,2048]{2,1,0:T(8,128)(2,1)} %param.7, bf16[2,2048,512]{2,1,0:T(8,128)(2,1)} %param.6, bf16[2,2,2048]{2,1,0:T(2,128)(2,1)S(1)} %all-gather.1), kind=kOutput, calls=%fused_computation | convolution fusion | flops 16795648 | bytes 8437760 | tf_op jit(solution)/shard_map/cef,efd->ced/dot_general | solution.py:22
  104.1 3.4 %psum.30 = f32[2,2,2048]{2,0,1:T(2,128)S(1)} all-reduce(f32[2,2,2048]{2,0,1:T(2,128)S(1)} %convolution_bitcast_fusion), channel_id=1, replica_groups=mesh['dp'=2,'seq'=8,'expert'=16] {'dp'}, use_global_device_ids=true, to_apply=%region_7.8 | all-reduce | flops 8192 | bytes 65536 | tf_op jit(solution)/shard_map/psum | solution.py:23
  107.5 27.6 %psum.31 = bf16[2,2,2048]{2,0,1:T(2,128)(2,1)S(1)} all-reduce(f32[2,2,2048]{2,0,1:T(2,128)S(1)} %psum.30), channel_id=1, replica_groups=mesh['dp'=2,'seq'=8,'expert'=16] {'seq'}, use_global_device_ids=true, to_apply=%region_8.9 | all-reduce | flops 8192 | bytes 49152 | tf_op jit(solution)/shard_map/psum | solution.py:23
  135.1 4.5 %fusion.15 = f32[1024,2048]{1,0:T(8,128)} fusion(bf16[1,2,2048]{2,0,1:T(2,128)(2,1)S(1)} %dynamic-slice_convert_fusion, f32[2,1024]{1,0:T(2,128)S(1)} %get-tuple-element.11, f32[1024]{0:T(1024)S(1)} %pmax.14), kind=kOutput, calls=%fused_computation.15 | convolution fusion | flops 8392704 | bytes 8409088 | tf_op jit(solution)/shard_map/dot_general | solution.py:28
  139.7 0.0 copy-start.1
  139.7 0.0 reduce-scatter.2.cloned.1.call-update
  139.7 0.6 copy-done.1
  140.3 0.6 dynamic-slice
  141.6 40.5 %all-reduce = f32[1024]{0:T(1024)S(1)} all-reduce(f32[1024]{0:T(1024)S(1)} %get-tuple-element.5), channel_id=4, replica_groups=mesh['dp'=2,'seq'=8,'expert'=16] {'expert'}, use_global_device_ids=true, to_apply=%region_11.12.clone | all-reduce | flops 1024 | bytes 8192
  182.0 0.1 dynamic-slice.1
  182.1 45.1 %reduce-scatter.2.cloned.1.call-done = f32[64,2048]{1,0:T(8,128)} async-done(((f32[1024,2048]{1,0:T(8,128)}), f32[64,2048]{1,0:T(8,128)}) %reduce-scatter.2.cloned.1.call-update) | async-done | bytes 524304 | tf_op jit(solution)/shard_map/reduce_scatter | solution.py:35
  227.2 1.8 divide_convert_fusion
  (1 shorter events, 0.0 us)
Async XLA Ops:
  6.5 0.7 copy-start
  6.5 220.6 %reduce-scatter.2.cloned.1.call-start = ((), (), s32[]{:S(2)}) async-start(), calls=%async_computation.1 | async-start | bytes 8912896 | tf_op jit(solution)/shard_map/reduce_scatter | solution.py:35
  139.7 0.7 copy-start.1
Sparse Core Ops, SparseCore 0:
  139.8 87.3 reduce-scatter.1
